TPU v7x, 512 devices: a whole 4x4x16 slice. The times are simulated.
512 devices in a mesh: seq: 16 (over y, x), dp: 32 (over z, core).
Axes of the slice: x: 4, y: 4, z: 16, core: 2. Of those that a mesh axis runs over, the one named last changes fastest.
Arguments:
- queries: bfloat16 [32, 2048, 2048], P('dp', 'seq'), may hold values from -30 to 30
- key_states: bfloat16 [32, 2048, 2048], P('dp', 'seq'), may hold values from -4.5 to 4.5
- value_states: bfloat16 [32, 2048, 2048], P('dp', 'seq'), may hold values from -6 to 6
- grad_out: bfloat16 [32, 2048, 2048], P('dp', 'seq'), may hold values from -18 to 18
- out_weight: bfloat16 [2048, 2048], P('dp'), may hold values from -0.125 to 0.125
- block_lists: int32 [16, 16, 8], P('seq'), may hold values from 0 to 15, as said below
- block_counts: int32 [16, 16], P('seq'), may hold values from 1 to 8, as said below
Outputs:
- query_grad: bfloat16 [32, 2048, 2048], P('dp', 'seq')
- key_grad: bfloat16 [32, 2048, 2048], P('dp', 'seq')
- value_grad: bfloat16 [32, 2048, 2048], P('dp', 'seq')
Inputs may be any that keep to these rules, and one draw needn't show every extreme that they name: The entries of one row block_lists[h, i, :] are distinct. `block_counts`: the counts of one head sum to at most 64; in every draw some head sums to exactly 64 and some query block uses all 8 entries.
All inputs are finite; a program needn't handle non-finite values.
Results may differ from a plain program's by a relative error of at most 0.0093.
Values may be sent and summed in bfloat16 or wider, within the bound.
A program may use at most 64 MiB of HBM per device.

v0:
```python
import jax
import jax.numpy as jnp
from jax import lax
from jax.sharding import PartitionSpec as P

HD = 128


def whole_rows(query_blocks, key_blocks, value_blocks, grad_blocks, lists_head, counts_head):
    nblocks, block_rows, head_width = query_blocks.shape
    kslots = lists_head.shape[1]
    group = 4
    score_scale = head_width ** (-0.5)

    def scan_step(running, block_slot):
        key_sum, value_sum = running
        query_group, grad_group, lists_group, counts_group = block_slot
        key_sets = key_blocks[lists_group]
        value_sets = value_blocks[lists_group]
        live_slots = jnp.arange(kslots, dtype=jnp.int32)[None, :] < counts_group[:, None]
        live_mask = live_slots[:, None, :, None]
        scores = (
            jnp.einsum("gqd,gjkd->gqjk", query_group, key_sets, preferred_element_type=jnp.float32)
            * score_scale
        )
        scores = jnp.where(live_mask, scores, -1e30)
        row_top = jnp.max(scores, axis=(2, 3), keepdims=True)
        weights = jnp.where(live_mask, jnp.exp(scores - row_top), 0.0)
        attn_probs = weights / jnp.sum(weights, axis=(2, 3), keepdims=True)
        probs_low = attn_probs.astype(jnp.bfloat16)
        attn_out = jnp.einsum(
            "gqjk,gjkd->gqd", probs_low, value_sets, preferred_element_type=jnp.float32
        )
        row_delta = jnp.sum(grad_group.astype(jnp.float32) * attn_out, axis=-1)
        prob_grad = jnp.einsum(
            "gqd,gjkd->gqjk", grad_group, value_sets, preferred_element_type=jnp.float32
        )
        score_low = (attn_probs * (prob_grad - row_delta[:, :, None, None])).astype(jnp.bfloat16)
        query_part = (
            jnp.einsum("gqjk,gjkd->gqd", score_low, key_sets, preferred_element_type=jnp.float32)
            * score_scale
        )
        key_parts = jnp.einsum(
            "gqjk,gqd->gjkd", score_low, query_group, preferred_element_type=jnp.float32
        )
        value_parts = jnp.einsum(
            "gqjk,gqd->gjkd", probs_low, grad_group, preferred_element_type=jnp.float32
        )
        key_sum = key_sum.at[lists_group].add(key_parts)
        value_sum = value_sum.at[lists_group].add(value_parts)
        return ((key_sum, value_sum), query_part.astype(jnp.bfloat16))

    def grouped(array):
        return array.reshape((nblocks // group, group) + array.shape[1:])

    empty_sum = jnp.zeros(query_blocks.shape, jnp.float32)
    final_state, query_part = lax.scan(
        scan_step,
        (empty_sum, empty_sum),
        (grouped(query_blocks), grouped(grad_blocks), grouped(lists_head), grouped(counts_head)),
    )
    key_sum, value_sum = final_state
    return (
        query_part.reshape(query_blocks.shape),
        (key_sum * score_scale).astype(jnp.bfloat16),
        value_sum.astype(jnp.bfloat16),
    )


def local(queries, key_states, value_states, grad_out, out_weight, block_lists, block_counts):
    tok_rows = queries.shape[1]
    model_width = queries.shape[2]
    head_total = model_width // HD
    head_local, nblocks, kslots = block_lists.shape

    def split_heads(matrix):
        return matrix.reshape(tok_rows, head_total, HD)

    def to_blocks(matrix):
        return jnp.moveaxis(matrix, 1, 0).reshape(head_local, nblocks, -1, HD)

    def from_blocks(blocks):
        return jnp.moveaxis(blocks.reshape(head_local, -1, HD), 0, 1)

    query_heads, key_heads, value_heads = (
        lax.all_to_all(split_heads(queries), "seq", split_axis=1, concat_axis=0, tiled=True),
        lax.all_to_all(split_heads(key_states), "seq", split_axis=1, concat_axis=0, tiled=True),
        lax.all_to_all(split_heads(value_states), "seq", split_axis=1, concat_axis=0, tiled=True),
    )
    query_blocks = to_blocks(query_heads)
    key_blocks = to_blocks(key_heads)
    value_blocks = to_blocks(value_heads)
    grad_rows = grad_out.reshape(tok_rows, model_width)
    attn_full = lax.dot_general(
        grad_rows,
        lax.all_gather(out_weight, "dp", axis=0, tiled=True),
        (((1,), (1,)), ((), ())),
        preferred_element_type=jnp.float32,
    )
    attn_low = attn_full.astype(jnp.bfloat16)
    grad_heads = lax.all_to_all(
        split_heads(attn_low), "seq", split_axis=1, concat_axis=0, tiled=True
    )
    grad_blocks = to_blocks(grad_heads)
    query_part, key_part, value_part = jax.vmap(whole_rows)(
        query_blocks, key_blocks, value_blocks, grad_blocks, block_lists, block_counts
    )
    returned = (
        lax.all_to_all(from_blocks(query_part), "seq", split_axis=0, concat_axis=1, tiled=True),
        lax.all_to_all(from_blocks(key_part), "seq", split_axis=0, concat_axis=1, tiled=True),
        lax.all_to_all(from_blocks(value_part), "seq", split_axis=0, concat_axis=1, tiled=True),
    )
    return (
        returned[0].reshape(1, tok_rows, model_width),
        returned[1].reshape(1, tok_rows, model_width),
        returned[2].reshape(1, tok_rows, model_width),
    )


def solution(mesh):
    placed = (
        P("dp", "seq", None),
        P("dp", "seq", None),
        P("dp", "seq", None),
        P("dp", "seq", None),
        P("dp", None),
        P("seq", None, None),
        P("seq", None),
    )
    return jax.shard_map(
        local,
        mesh=mesh,
        in_specs=placed,
        out_specs=(P("dp", "seq", None), P("dp", "seq", None), P("dp", "seq", None)),
        check_vma=False,
    )
```

profile of v0, /device:TPU:32, one launch (start us, length us, event | category | flops | bytes accessed | tf_op | source)
XLA Modules:
  0.0 279.4 jit_solution(4677492128257543968)
XLA Ops:
  10.0 7.1 %all-to-all-start = ((bf16[128,16,128]{2,0,1:T(8,128)(2,1)}), bf16[128,16,128]{2,0,1:T(8,128)(2,1)}, u32[]{:S(2)}, u32[]{:S(2)}) async-start(bf16[128,16,128]{2,0,1:T(8,128)(2,1)} %copy.81), calls=%async_computation | async-start | bytes 1048576 | tf_op jit(solution)/shard_map/all_to_all | solution.py:86
  18.1 10.6 %all-to-all-done = bf16[128,16,128]{2,0,1:T(8,128)(2,1)} async-done(((bf16[128,16,128]{2,0,1:T(8,128)(2,1)}), bf16[128,16,128]{2,0,1:T(8,128)(2,1)}, u32[]{:S(2)}, u32[]{:S(2)}) %all-to-all-start) | async-done | bytes 524320 | tf_op jit(solution)/shard_map/all_to_all | solution.py:86
  28.7 3.6 %all-to-all-start.1 = ((bf16[128,16,128]{0,2,1:T(8,128)(2,1)}), bf16[128,16,128]{0,2,1:T(8,128)(2,1)S(1)}, u32[]{:S(2)}, u32[]{:S(2)}) async-start(bf16[128,16,128]{0,2,1:T(8,128)(2,1)} %bitcast.29), calls=%async_computation.1 | async-start | bytes 1048576 | tf_op jit(solution)/shard_map/all_to_all | solution.py:87
  33.3 9.4 %all-to-all-done.1 = bf16[128,16,128]{0,2,1:T(8,128)(2,1)S(1)} async-done(((bf16[128,16,128]{0,2,1:T(8,128)(2,1)}), bf16[128,16,128]{0,2,1:T(8,128)(2,1)S(1)}, u32[]{:S(2)}, u32[]{:S(2)}) %all-to-all-start.1) | async-done | bytes 524320 | tf_op jit(solution)/shard_map/all_to_all | solution.py:87
  42.7 3.6 %all-to-all-start.3 = ((bf16[128,16,128]{0,2,1:T(8,128)(2,1)}), bf16[128,16,128]{0,2,1:T(8,128)(2,1)S(1)}, u32[]{:S(2)}, u32[]{:S(2)}) async-start(bf16[128,16,128]{0,2,1:T(8,128)(2,1)} %bitcast.38), calls=%async_computation.3 | async-start | bytes 1048576 | tf_op jit(solution)/shard_map/all_to_all | solution.py:88
  46.3 46.6 %all-gather.2.cloned.1.call-done = bf16[2048,2048]{1,0:T(8,128)(2,1)} async-done(((bf16[64,2048]{1,0:T(8,128)(2,1)}), bf16[2048,2048]{1,0:T(8,128)(2,1)}) %all-gather.2.cloned.1.call-update) | async-done | bytes 8388624 | tf_op jit(solution)/shard_map/all_gather | solution.py:96
  92.9 6.3 %fusion.29 = bf16[16,16,8,128]{3,2,1,0:T(8,128)(2,1)S(1)} fusion(bf16[2048,2048]{1,0:T(8,128)(2,1)} %all-gather.2.cloned.1.call-done, bf16[1,128,2048]{2,1,0:T(8,128)(2,1)S(1)} %copy-done), kind=kOutput, calls=%fused_computation.43 | convolution fusion | flops 1074003968 | bytes 9437184 | tf_op jit(solution)/shard_map/dot_general | solution.py:94
  100.1 6.9 %all-to-all-start.2 = ((bf16[128,16,128]{2,0,1:T(8,128)(2,1)}), bf16[128,16,128]{2,0,1:T(8,128)(2,1)}, u32[]{:S(2)}, u32[]{:S(2)}) async-start(bf16[128,16,128]{2,0,1:T(8,128)(2,1)} %bitcast.120), calls=%async_computation.2 | async-start | bytes 1048576 | tf_op jit(solution)/shard_map/all_to_all | solution.py:101
  109.7 9.3 %all-to-all-done.2 = bf16[128,16,128]{2,0,1:T(8,128)(2,1)} async-done(((bf16[128,16,128]{2,0,1:T(8,128)(2,1)}), bf16[128,16,128]{2,0,1:T(8,128)(2,1)}, u32[]{:S(2)}, u32[]{:S(2)}) %all-to-all-start.2) | async-done | bytes 524320 | tf_op jit(solution)/shard_map/all_to_all | solution.py:101
  121.2 104.3 %while.14 = (s32[]{:T(128)}, f32[1,16,128,128]{3,2,1,0:T(8,128)}, f32[1,16,128,128]{3,2,1,0:T(8,128)}, bf16[4,1,4,128,128]{4,3,2,1,0:T(8,128)(2,1)}, s32[4,1,4,8...) while((s32[]{:T(128)}, f32[1,16,128,128]{3,2,1,0:T(8,128)}, ...), condition=%wide.region_6.7_spmd, body=%wide.region_0.6_spmd.sunk | while | flops 821361536 | bytes 47997756 | solution.py:57
  133.4 6.1 %scatter_fusion.1 = f32[16,128,128]{2,1,0:T(8,128)} fusion(f32[16,128,128]{2,1,0:T(8,128)} %bitcast.168, s32[32]{0:T(128)S(1)} %reshape.276, f32[32,128,128]{2,1,0:T(8,128)S(1)} %bitcast.174), kind=kCustom, calls=%fused_computation.3.clone.1 | custom fusion | flops 524288 | bytes 6291584 | tf_op jit(solution)/shard_map/vmap()/while/body/eval_jaxpr/scatter-add | solution.py:50
  141.2 6.1 %scatter_fusion = f32[16,128,128]{2,1,0:T(8,128)} fusion(f32[16,128,128]{2,1,0:T(8,128)} %bitcast.163, s32[32]{0:T(128)S(1)} %reshape.276, f32[32,128,128]{2,1,0:T(8,128)S(1)} %bitcast.173), kind=kCustom, calls=%fused_computation.2.clone.1 | custom fusion | flops 524288 | bytes 6291584 | tf_op jit(solution)/shard_map/vmap()/while/body/eval_jaxpr/scatter-add | solution.py:49
  159.5 6.1 %scatter_fusion.1 = f32[16,128,128]{2,1,0:T(8,128)} fusion(f32[16,128,128]{2,1,0:T(8,128)} %bitcast.168, s32[32]{0:T(128)S(1)} %reshape.276, f32[32,128,128]{2,1,0:T(8,128)S(1)} %bitcast.174), kind=kCustom, calls=%fused_computation.3.clone.1 | custom fusion | flops 524288 | bytes 6291584 | tf_op jit(solution)/shard_map/vmap()/while/body/eval_jaxpr/scatter-add | solution.py:50
  167.3 6.1 %scatter_fusion = f32[16,128,128]{2,1,0:T(8,128)} fusion(f32[16,128,128]{2,1,0:T(8,128)} %bitcast.163, s32[32]{0:T(128)S(1)} %reshape.276, f32[32,128,128]{2,1,0:T(8,128)S(1)} %bitcast.173), kind=kCustom, calls=%fused_computation.2.clone.1 | custom fusion | flops 524288 | bytes 6291584 | tf_op jit(solution)/shard_map/vmap()/while/body/eval_jaxpr/scatter-add | solution.py:49
  185.6 6.2 %scatter_fusion.1 = f32[16,128,128]{2,1,0:T(8,128)} fusion(f32[16,128,128]{2,1,0:T(8,128)} %bitcast.168, s32[32]{0:T(128)S(1)} %reshape.276, f32[32,128,128]{2,1,0:T(8,128)S(1)} %bitcast.174), kind=kCustom, calls=%fused_computation.3.clone.1 | custom fusion | flops 524288 | bytes 6291584 | tf_op jit(solution)/shard_map/vmap()/while/body/eval_jaxpr/scatter-add | solution.py:50
  193.4 6.1 %scatter_fusion = f32[16,128,128]{2,1,0:T(8,128)} fusion(f32[16,128,128]{2,1,0:T(8,128)} %bitcast.163, s32[32]{0:T(128)S(1)} %reshape.276, f32[32,128,128]{2,1,0:T(8,128)S(1)} %bitcast.173), kind=kCustom, calls=%fused_computation.2.clone.1 | custom fusion | flops 524288 | bytes 6291584 | tf_op jit(solution)/shard_map/vmap()/while/body/eval_jaxpr/scatter-add | solution.py:49
  211.6 6.1 %scatter_fusion.1 = f32[16,128,128]{2,1,0:T(8,128)} fusion(f32[16,128,128]{2,1,0:T(8,128)} %bitcast.168, s32[32]{0:T(128)S(1)} %reshape.276, f32[32,128,128]{2,1,0:T(8,128)S(1)} %bitcast.174), kind=kCustom, calls=%fused_computation.3.clone.1 | custom fusion | flops 524288 | bytes 6291584 | tf_op jit(solution)/shard_map/vmap()/while/body/eval_jaxpr/scatter-add | solution.py:50
  219.4 6.1 %scatter_fusion = f32[16,128,128]{2,1,0:T(8,128)} fusion(f32[16,128,128]{2,1,0:T(8,128)} %bitcast.163, s32[32]{0:T(128)S(1)} %reshape.276, f32[32,128,128]{2,1,0:T(8,128)S(1)} %bitcast.173), kind=kCustom, calls=%fused_computation.2.clone.1 | custom fusion | flops 524288 | bytes 6291584 | tf_op jit(solution)/shard_map/vmap()/while/body/eval_jaxpr/scatter-add | solution.py:49
  229.0 3.8 %all-to-all-start.4 = ((bf16[16,2,8192]{2,1,0:T(2,128)(2,1)}), bf16[16,2,8192]{2,1,0:T(2,128)(2,1)S(1)}, u32[]{:S(2)}, u32[]{:S(2)}) async-start(bf16[16,2,8192]{2,1,0:T(2,128)(2,1)} %reshape.252), calls=%async_computation.4 | async-start | bytes 1048576 | tf_op jit(solution)/shard_map/all_to_all | solution.py:109
  236.1 7.3 %all-to-all-done.4 = bf16[16,2,8192]{2,1,0:T(2,128)(2,1)S(1)} async-done(((bf16[16,2,8192]{2,1,0:T(2,128)(2,1)}), bf16[16,2,8192]{2,1,0:T(2,128)(2,1)S(1)}, u32[]{:S(2)}, u32[]{:S(2)}) %all-to-all-start.4) | async-done | bytes 524320 | tf_op jit(solution)/shard_map/all_to_all | solution.py:109
  243.3 3.6 %all-to-all-start.5 = ((bf16[16,2,8192]{2,1,0:T(2,128)(2,1)}), bf16[16,2,8192]{2,1,0:T(2,128)(2,1)S(1)}, u32[]{:S(2)}, u32[]{:S(2)}) async-start(bf16[16,2,8192]{2,1,0:T(2,128)(2,1)} %reshape.254), calls=%async_computation.5 | async-start | bytes 1048576 | tf_op jit(solution)/shard_map/all_to_all | solution.py:110
  250.2 6.8 %all-to-all-done.5 = bf16[16,2,8192]{2,1,0:T(2,128)(2,1)S(1)} async-done(((bf16[16,2,8192]{2,1,0:T(2,128)(2,1)}), bf16[16,2,8192]{2,1,0:T(2,128)(2,1)S(1)}, u32[]{:S(2)}, u32[]{:S(2)}) %all-to-all-start.5) | async-done | bytes 524320 | tf_op jit(solution)/shard_map/all_to_all | solution.py:110
  257.0 3.6 %all-to-all-start.6 = ((bf16[16,2,8192]{2,1,0:T(2,128)(2,1)}), bf16[16,2,8192]{2,1,0:T(2,128)(2,1)S(1)}, u32[]{:S(2)}, u32[]{:S(2)}) async-start(bf16[16,2,8192]{2,1,0:T(2,128)(2,1)} %reshape.256), calls=%async_computation.6 | async-start | bytes 1048576 | tf_op jit(solution)/shard_map/all_to_all | solution.py:111
  264.4 6.3 %all-to-all-done.6 = bf16[16,2,8192]{2,1,0:T(2,128)(2,1)S(1)} async-done(((bf16[16,2,8192]{2,1,0:T(2,128)(2,1)}), bf16[16,2,8192]{2,1,0:T(2,128)(2,1)S(1)}, u32[]{:S(2)}, u32[]{:S(2)}) %all-to-all-start.6) | async-done | bytes 524320 | tf_op jit(solution)/shard_map/all_to_all | solution.py:111
  (128 shorter events, 81.5 us)
Async XLA Ops:
  7.2 85.7 %copy-start = (bf16[1,128,2048]{2,1,0:T(8,128)(2,1)S(1)}, bf16[1,128,2048]{2,1,0:T(8,128)(2,1)}, u32[]{:S(2)}) copy-start(bf16[1,128,2048]{2,1,0:T(8,128)(2,1)} %param.12) | copy-start | bytes 1572868
  7.2 9.9 %copy-start.3 = (bf16[1,128,2048]{2,1,0:T(8,128)(2,1)S(1)}, bf16[1,128,2048]{2,1,0:T(8,128)(2,1)}, u32[]{:S(2)}) copy-start(bf16[1,128,2048]{2,1,0:T(8,128)(2,1)} %param.10) | copy-start | bytes 1572868
  7.2 85.7 %all-gather.2.cloned.1.call-start = ((), (), s32[]{:S(2)}) async-start(), calls=%async_computation.7 | async-start | bytes 8650752 | tf_op jit(solution)/shard_map/all_gather | solution.py:96
  9.1 23.2 %copy-start.4 = (bf16[1,128,2048]{2,1,0:T(8,128)(2,1)S(1)}, bf16[1,128,2048]{2,1,0:T(8,128)(2,1)}, u32[]{:S(2)}) copy-start(bf16[1,128,2048]{2,1,0:T(8,128)(2,1)} %param.11) | copy-start | bytes 1572868
  10.0 18.7 %all-to-all-start = ((bf16[128,16,128]{2,0,1:T(8,128)(2,1)}), bf16[128,16,128]{2,0,1:T(8,128)(2,1)}, u32[]{:S(2)}, u32[]{:S(2)}) async-start(bf16[128,16,128]{2,0,1:T(8,128)(2,1)} %copy.81), calls=%async_computation | async-start | bytes 1048576 | tf_op jit(solution)/shard_map/all_to_all | solution.py:86
  28.7 14.0 %all-to-all-start.1 = ((bf16[128,16,128]{0,2,1:T(8,128)(2,1)}), bf16[128,16,128]{0,2,1:T(8,128)(2,1)S(1)}, u32[]{:S(2)}, u32[]{:S(2)}) async-start(bf16[128,16,128]{0,2,1:T(8,128)(2,1)} %bitcast.29), calls=%async_computation.1 | async-start | bytes 1048576 | tf_op jit(solution)/shard_map/all_to_all | solution.py:87
  42.7 57.4 %all-to-all-start.3 = ((bf16[128,16,128]{0,2,1:T(8,128)(2,1)}), bf16[128,16,128]{0,2,1:T(8,128)(2,1)S(1)}, u32[]{:S(2)}, u32[]{:S(2)}) async-start(bf16[128,16,128]{0,2,1:T(8,128)(2,1)} %bitcast.38), calls=%async_computation.3 | async-start | bytes 1048576 | tf_op jit(solution)/shard_map/all_to_all | solution.py:88
  99.2 8.4 %copy-start.6 = (s32[1,16]{1,0:T(1,128)S(1)}, s32[1,16]{1,0:T(1,128)}, u32[]{:S(2)}) copy-start(s32[1,16]{1,0:T(1,128)} %param.15) | copy-start | bytes 196
  99.2 9.1 %copy-start.5 = (s32[1,16,8]{1,2,0:T(8,128)S(1)}, s32[1,16,8]{1,2,0:T(8,128)}, u32[]{:S(2)}) copy-start(s32[1,16,8]{1,2,0:T(8,128)} %param.14) | copy-start | bytes 1540
  100.1 18.9 %all-to-all-start.2 = ((bf16[128,16,128]{2,0,1:T(8,128)(2,1)}), bf16[128,16,128]{2,0,1:T(8,128)(2,1)}, u32[]{:S(2)}, u32[]{:S(2)}) async-start(bf16[128,16,128]{2,0,1:T(8,128)(2,1)} %bitcast.120), calls=%async_computation.2 | async-start | bytes 1048576 | tf_op jit(solution)/shard_map/all_to_all | solution.py:101
  125.0 2.1 copy-start.2
  130.6 2.8 %copy-start.1 = (bf16[4,128,8,128]{1,3,2,0:T(8,128)(2,1)}, bf16[4,128,8,128]{1,3,2,0:T(8,128)(2,1)S(1)}, u32[]{:S(2)}) copy-start(bf16[4,128,8,128]{1,3,2,0:T(8,128)(2,1)S(1)} %multiply_convert_fusion.3) | copy-start | bytes 3145732 | tf_op jit(solution)/shard_map/vmap()/while
  151.1 2.1 copy-start.2
  156.7 2.8 %copy-start.1 = (bf16[4,128,8,128]{1,3,2,0:T(8,128)(2,1)}, bf16[4,128,8,128]{1,3,2,0:T(8,128)(2,1)S(1)}, u32[]{:S(2)}) copy-start(bf16[4,128,8,128]{1,3,2,0:T(8,128)(2,1)S(1)} %multiply_convert_fusion.3) | copy-start | bytes 3145732 | tf_op jit(solution)/shard_map/vmap()/while
  177.1 2.1 copy-start.2
  182.8 2.8 %copy-start.1 = (bf16[4,128,8,128]{1,3,2,0:T(8,128)(2,1)}, bf16[4,128,8,128]{1,3,2,0:T(8,128)(2,1)S(1)}, u32[]{:S(2)}) copy-start(bf16[4,128,8,128]{1,3,2,0:T(8,128)(2,1)S(1)} %multiply_convert_fusion.3) | copy-start | bytes 3145732 | tf_op jit(solution)/shard_map/vmap()/while
  203.2 2.1 copy-start.2
  208.8 2.8 %copy-start.1 = (bf16[4,128,8,128]{1,3,2,0:T(8,128)(2,1)}, bf16[4,128,8,128]{1,3,2,0:T(8,128)(2,1)S(1)}, u32[]{:S(2)}) copy-start(bf16[4,128,8,128]{1,3,2,0:T(8,128)(2,1)S(1)} %multiply_convert_fusion.3) | copy-start | bytes 3145732 | tf_op jit(solution)/shard_map/vmap()/while
  229.0 14.4 %all-to-all-start.4 = ((bf16[16,2,8192]{2,1,0:T(2,128)(2,1)}), bf16[16,2,8192]{2,1,0:T(2,128)(2,1)S(1)}, u32[]{:S(2)}, u32[]{:S(2)}) async-start(bf16[16,2,8192]{2,1,0:T(2,128)(2,1)} %reshape.252), calls=%async_computation.4 | async-start | bytes 1048576 | tf_op jit(solution)/shard_map/all_to_all | solution.py:109
  243.3 13.7 %all-to-all-start.5 = ((bf16[16,2,8192]{2,1,0:T(2,128)(2,1)}), bf16[16,2,8192]{2,1,0:T(2,128)(2,1)S(1)}, u32[]{:S(2)}, u32[]{:S(2)}) async-start(bf16[16,2,8192]{2,1,0:T(2,128)(2,1)} %reshape.254), calls=%async_computation.5 | async-start | bytes 1048576 | tf_op jit(solution)/shard_map/all_to_all | solution.py:110
  257.0 13.7 %all-to-all-start.6 = ((bf16[16,2,8192]{2,1,0:T(2,128)(2,1)}), bf16[16,2,8192]{2,1,0:T(2,128)(2,1)S(1)}, u32[]{:S(2)}, u32[]{:S(2)}) async-start(bf16[16,2,8192]{2,1,0:T(2,128)(2,1)} %reshape.256), calls=%async_computation.6 | async-start | bytes 1048576 | tf_op jit(solution)/shard_map/all_to_all | solution.py:111
Sparse Core Ops, SparseCore 0:
  10.1 82.7 all-gather.1
where the time goes:
time: 282 us; the launch traced here: 279 us
  waiting for transfers between devices  97 us (34%)
  other arithmetic  59.2 us (21%)
  matrix products  43.9 us (16%)
  local copies, waits for them, and re-layouts  32.8 us (12%)
  starting transfers between devices  32.1 us (11%)
  between operations  14.3 us (5%)
    all_gather x1, waiting for transfers between devices, local(): lax.all_gather(out_weight, 'dp', axis=0, tiled=True)  46.6 us
    scatter-add x4, other arithmetic, scan_step(): value_sum = value_sum.at[lists_group].add(value_parts)  24.5 us
    scatter-add x8, other arithmetic, scan_step(): key_sum = key_sum.at[lists_group].add(key_parts)  24.4 us
    unnamed x27, local copies, waits for them, and re-layouts  11.3 us
    gather x4, local copies, waits for them, and re-layouts, scan_step(): value_sets = value_blocks[lists_group]  10.9 us
    all_to_all x1, waiting for transfers between devices, local(): lax.all_to_all(split_heads(queries), 'seq', split_axis=1, concat_axis=0,...  10.6 us
    all_to_all x1, waiting for transfers between devices, local(): lax.all_to_all(split_heads(key_states), 'seq', split_axis=1, concat_axis=...  9.42 us
    all_to_all x1, waiting for transfers between devices, local(): lax.all_to_all(split_heads(attn_low), 'seq', split_axis=1, concat_axis=0,...  9.34 us
  transfers between devices with their start and end apart: 8, of which 7 were waited for; matrix products, arithmetic and copies ran while one was open for 9% of the time, Pallas kernels for 0%

commit v1 on v0

--- a/solution.py
+++ b/solution.py
@@ -93,7 +93,9 @@
     grad_rows = grad_out.reshape(tok_rows, model_width)
     attn_full = lax.dot_general(
         grad_rows,
-        lax.all_gather(out_weight, "dp", axis=0, tiled=True),
+        jnp.concatenate(
+            lax.all_to_all(jnp.stack([out_weight] * lax.axis_size("dp")), "dp", 0, 0), axis=0
+        ),
         (((1,), (1,)), ((), ())),
         preferred_element_type=jnp.float32,
     )

time: 282 us -> 625 us (2.22)
  waiting for transfers between devices: 97 us -> 414 us
  matrix products: 43.9 us -> 63.4 us
  blocking collectives: 0 us -> 13.7 us
  between operations: 14.3 us -> 0.9 us
  starting transfers between devices: 32.1 us -> 41.3 us
    all_to_all x1, waiting for transfers between devices: 9.42 us -> 369 us  [local(): lax.all_to_all(jnp.stack([out_weight] * lax.axis_size('dp')), 'dp', 0, 0)]
    all_gather x1 -> x0, waiting for transfers between devices: 46.6 us -> none  [local(): lax.all_gather(out_weight, 'dp', axis=0, tiled=True)]
    all_to_all x0 -> x1, blocking collectives: none -> 13.7 us  [local(): lax.all_to_all(split_heads(key_states), 'seq', split_axis=1, concat_axis=...]
    all_to_all x1, starting transfers between devices: 3.57 us -> 15.5 us  [local(): lax.all_to_all(jnp.stack([out_weight] * lax.axis_size('dp')), 'dp', 0, 0)]
  transfers between devices with their start and end apart: 8 -> 7, of which waited for: 7 -> 7; matrix products, arithmetic and copies ran while one was open for 9% -> 3% of each run, Pallas kernels for 0% -> 0%
where the time goes in v1:
time: 625 us; the launch traced here: 623 us
  waiting for transfers between devices  414 us (66%)
  matrix products  63.4 us (10%)
  other arithmetic  54.3 us (9%)
  starting transfers between devices  41.3 us (7%)
  local copies, waits for them, and re-layouts  35.4 us (6%)
  blocking collectives  13.7 us (2%)
    all_to_all x1, waiting for transfers between devices, local(): lax.all_to_all(jnp.stack([out_weight] * lax.axis_size('dp')), 'dp', 0, 0)  369 us
    scatter-add x4, other arithmetic, scan_step(): value_sum = value_sum.at[lists_group].add(value_parts)  27.9 us
    scatter-add x8, other arithmetic, scan_step(): key_sum = key_sum.at[lists_group].add(key_parts)  18.7 us
    all_to_all x1, starting transfers between devices, local(): lax.all_to_all(jnp.stack([out_weight] * lax.axis_size('dp')), 'dp', 0, 0)  15.5 us
    all_to_all x1, blocking collectives, local(): lax.all_to_all(split_heads(key_states), 'seq', split_axis=1, concat_axis=...  13.7 us
  transfers between devices with their start and end apart: 7, of which 7 were waited for; matrix products, arithmetic and copies ran while one was open for 3% of the time, Pallas kernels for 0%

profile of v1, /device:TPU:32, one launch (start us, length us, event | category | flops | bytes accessed | tf_op | source)
XLA Modules:
  0.0 622.9 jit_solution(9810895889124533939)
XLA Ops:
  2.8 7.0 %all-to-all-start = ((bf16[128,16,128]{2,0,1:T(8,128)(2,1)}), bf16[128,16,128]{2,0,1:T(8,128)(2,1)S(1)}, u32[]{:S(2)}, u32[]{:S(2)}) async-start(bf16[128,16,128]{2,0,1:T(8,128)(2,1)} %copy.81), calls=%async_computation | async-start | bytes 1048576 | tf_op jit(solution)/shard_map/all_to_all | solution.py:86
  10.2 11.2 %all-to-all-done = bf16[128,16,128]{2,0,1:T(8,128)(2,1)S(1)} async-done(((bf16[128,16,128]{2,0,1:T(8,128)(2,1)}), bf16[128,16,128]{2,0,1:T(8,128)(2,1)S(1)}, u32[]{:S(2)}, u32[]{:S(2)}) %all-to-all-start) | async-done | bytes 524320 | tf_op jit(solution)/shard_map/all_to_all | solution.py:86
  21.4 13.7 %all_to_all.110 = bf16[128,16,128]{0,2,1:T(8,128)(2,1)S(1)} all-to-all(bf16[128,16,128]{0,2,1:T(8,128)(2,1)S(1)} %bitcast.190), channel_id=1, replica_groups=mesh['seq'=16,'dp'=32] {'seq'}, dimensions={1} | all-to-all | bytes 1048576 | tf_op jit(solution)/shard_map/all_to_all | solution.py:87
  35.1 4.3 stack.2
  39.4 15.5 %all-to-all-start.2 = ((bf16[32,64,2048]{2,1,0:T(8,128)(2,1)}), bf16[32,64,2048]{2,1,0:T(8,128)(2,1)}, u32[]{:S(2)}, u32[]{:S(2)}) async-start(bf16[32,64,2048]{2,1,0:T(8,128)(2,1)} %stack.2), calls=%async_computation.2 | async-start | bytes 16777216 | tf_op jit(solution)/shard_map/all_to_all | solution.py:97
  56.0 368.9 %all-to-all-done.2 = bf16[32,64,2048]{2,1,0:T(8,128)(2,1)} async-done(((bf16[32,64,2048]{2,1,0:T(8,128)(2,1)}), bf16[32,64,2048]{2,1,0:T(8,128)(2,1)}, u32[]{:S(2)}, u32[]{:S(2)}) %all-to-all-start.2) | async-done | bytes 8388640 | tf_op jit(solution)/shard_map/all_to_all | solution.py:97
  424.9 3.6 all-to-all-start.4
  428.5 6.3 %fusion.29 = bf16[16,16,8,128]{3,2,1,0:T(8,128)(2,1)S(1)} fusion(bf16[2048,2048]{1,0:T(8,128)(2,1)} %bitcast.34, bf16[1,128,2048]{2,1,0:T(8,128)(2,1)S(1)} %copy-done), kind=kOutput, calls=%fused_computation.43 | convolution fusion | flops 1074003968 | bytes 9437184 | tf_op jit(solution)/shard_map/dot_general | solution.py:94
  435.7 4.2 all-to-all-done.4
  439.9 4.4 all-to-all-start.3
  447.0 7.7 %all-to-all-done.3 = bf16[128,16,128]{2,0,1:T(8,128)(2,1)} async-done(((bf16[128,16,128]{2,0,1:T(8,128)(2,1)}), bf16[128,16,128]{2,0,1:T(8,128)(2,1)}, u32[]{:S(2)}, u32[]{:S(2)}) %all-to-all-start.3) | async-done | bytes 524320 | tf_op jit(solution)/shard_map/all_to_all | solution.py:103
  455.9 121.5 %while.14 = (s32[]{:T(128)}, f32[1,16,128,128]{3,2,1,0:T(8,128)S(1)}, f32[1,16,128,128]{3,2,1,0:T(8,128)}, bf16[4,1,4,128,128]{4,3,2,1,0:T(8,128)(2,1)}, s32[4,1...) while((s32[]{:T(128)}, ...), condition=%wide.region_6.7_spmd, body=%wide.region_0.6_spmd.sunk | while | flops 821361536 | bytes 64777560 | solution.py:57
  461.9 7.0 %scatter_fusion.1 = f32[16,128,128]{2,1,0:T(8,128)} fusion(f32[16,128,128]{2,1,0:T(8,128)} %bitcast.177, s32[32]{0:T(128)S(1)} %reshape.282, f32[32,128,128]{2,1,0:T(8,128)} %bitcast.179), kind=kCustom, calls=%fused_computation.3.clone.1 | custom fusion | flops 524288 | bytes 6291584 | tf_op jit(solution)/shard_map/vmap()/while/body/eval_jaxpr/scatter-add | solution.py:50
  479.2 4.7 scatter_fusion
  492.3 7.0 %scatter_fusion.1 = f32[16,128,128]{2,1,0:T(8,128)} fusion(f32[16,128,128]{2,1,0:T(8,128)} %bitcast.177, s32[32]{0:T(128)S(1)} %reshape.282, f32[32,128,128]{2,1,0:T(8,128)} %bitcast.179), kind=kCustom, calls=%fused_computation.3.clone.1 | custom fusion | flops 524288 | bytes 6291584 | tf_op jit(solution)/shard_map/vmap()/while/body/eval_jaxpr/scatter-add | solution.py:50
  509.6 4.7 scatter_fusion
  522.7 7.0 %scatter_fusion.1 = f32[16,128,128]{2,1,0:T(8,128)} fusion(f32[16,128,128]{2,1,0:T(8,128)} %bitcast.177, s32[32]{0:T(128)S(1)} %reshape.282, f32[32,128,128]{2,1,0:T(8,128)} %bitcast.179), kind=kCustom, calls=%fused_computation.3.clone.1 | custom fusion | flops 524288 | bytes 6291584 | tf_op jit(solution)/shard_map/vmap()/while/body/eval_jaxpr/scatter-add | solution.py:50
  539.9 4.7 scatter_fusion
  553.0 7.0 %scatter_fusion.1 = f32[16,128,128]{2,1,0:T(8,128)} fusion(f32[16,128,128]{2,1,0:T(8,128)} %bitcast.177, s32[32]{0:T(128)S(1)} %reshape.282, f32[32,128,128]{2,1,0:T(8,128)} %bitcast.179), kind=kCustom, calls=%fused_computation.3.clone.1 | custom fusion | flops 524288 | bytes 6291584 | tf_op jit(solution)/shard_map/vmap()/while/body/eval_jaxpr/scatter-add | solution.py:50
  570.3 4.7 scatter_fusion
  585.6 8.1 %all-to-all-done.6 = bf16[16,2,8192]{2,1,0:T(2,128)(2,1)S(1)} async-done(((bf16[16,2,8192]{2,1,0:T(2,128)(2,1)}), bf16[16,2,8192]{2,1,0:T(2,128)(2,1)S(1)}, u32[]{:S(2)}, u32[]{:S(2)}) %all-to-all-start.6) | async-done | bytes 524320 | tf_op jit(solution)/shard_map/all_to_all | solution.py:112
  600.2 7.1 %all-to-all-done.7 = bf16[16,2,8192]{2,1,0:T(2,128)(2,1)S(1)} async-done(((bf16[16,2,8192]{2,1,0:T(2,128)(2,1)}), bf16[16,2,8192]{2,1,0:T(2,128)(2,1)S(1)}, u32[]{:S(2)}, u32[]{:S(2)}) %all-to-all-start.7) | async-done | bytes 524320 | tf_op jit(solution)/shard_map/all_to_all | solution.py:113
  607.3 3.6 all-to-all-start.5
  614.7 6.3 %all-to-all-done.5 = bf16[16,2,8192]{2,1,0:T(2,128)(2,1)S(1)} async-done(((bf16[16,2,8192]{2,1,0:T(2,128)(2,1)}), bf16[16,2,8192]{2,1,0:T(2,128)(2,1)S(1)}, u32[]{:S(2)}, u32[]{:S(2)}) %all-to-all-start.5) | async-done | bytes 524320 | tf_op jit(solution)/shard_map/all_to_all | solution.py:111
  (149 shorter events, 103.2 us)
Async XLA Ops:
  0.6 427.8 %copy-start = (bf16[1,128,2048]{2,1,0:T(8,128)(2,1)S(1)}, bf16[1,128,2048]{2,1,0:T(8,128)(2,1)}, u32[]{:S(2)}) copy-start(bf16[1,128,2048]{2,1,0:T(8,128)(2,1)} %param.12) | copy-start | bytes 1572868
  0.6 9.2 %copy-start.7 = (bf16[1,128,2048]{2,1,0:T(8,128)(2,1)S(1)}, bf16[1,128,2048]{2,1,0:T(8,128)(2,1)}, u32[]{:S(2)}) copy-start(bf16[1,128,2048]{2,1,0:T(8,128)(2,1)} %param.10) | copy-start | bytes 1572868
  1.9 33.2 %copy-start.9 = (bf16[64,2048]{1,0:T(8,128)(2,1)S(1)}, bf16[64,2048]{1,0:T(8,128)(2,1)}, u32[]{:S(2)}) copy-start(bf16[64,2048]{1,0:T(8,128)(2,1)} %param.13) | copy-start | bytes 786436
  2.8 18.6 %all-to-all-start = ((bf16[128,16,128]{2,0,1:T(8,128)(2,1)}), bf16[128,16,128]{2,0,1:T(8,128)(2,1)S(1)}, u32[]{:S(2)}, u32[]{:S(2)}) async-start(bf16[128,16,128]{2,0,1:T(8,128)(2,1)} %copy.81), calls=%async_computation | async-start | bytes 1048576 | tf_op jit(solution)/shard_map/all_to_all | solution.py:86
  21.4 18.0 %copy-start.6 = (bf16[128,16,128]{2,0,1:T(8,128)(2,1)}, bf16[128,16,128]{2,0,1:T(8,128)(2,1)S(1)}, u32[]{:S(2)}) copy-start(bf16[128,16,128]{2,0,1:T(8,128)(2,1)S(1)} %all-to-all-done) | copy-start | bytes 1572868
  39.4 15.6 %copy-start.8 = (bf16[1,128,2048]{2,1,0:T(8,128)(2,1)S(1)}, bf16[1,128,2048]{2,1,0:T(8,128)(2,1)}, u32[]{:S(2)}) copy-start(bf16[1,128,2048]{2,1,0:T(8,128)(2,1)} %param.11) | copy-start | bytes 1572868
  39.4 385.5 %all-to-all-start.2 = ((bf16[32,64,2048]{2,1,0:T(8,128)(2,1)}), bf16[32,64,2048]{2,1,0:T(8,128)(2,1)}, u32[]{:S(2)}, u32[]{:S(2)}) async-start(bf16[32,64,2048]{2,1,0:T(8,128)(2,1)} %stack.2), calls=%async_computation.2 | async-start | bytes 16777216 | tf_op jit(solution)/shard_map/all_to_all | solution.py:97
  424.9 15.1 %all-to-all-start.4 = ((bf16[128,16,128]{0,2,1:T(8,128)(2,1)}), bf16[128,16,128]{0,2,1:T(8,128)(2,1)S(1)}, u32[]{:S(2)}, u32[]{:S(2)}) async-start(bf16[128,16,128]{0,2,1:T(8,128)(2,1)} %bitcast.39), calls=%async_computation.4 | async-start | bytes 1048576 | tf_op jit(solution)/shard_map/all_to_all | solution.py:88
  434.8 10.2 %copy-start.11 = (s32[1,16]{1,0:T(1,128)S(1)}, s32[1,16]{1,0:T(1,128)}, u32[]{:S(2)}) copy-start(s32[1,16]{1,0:T(1,128)} %param.15) | copy-start | bytes 196
  434.8 10.8 %copy-start.10 = (s32[1,16,8]{1,2,0:T(8,128)S(1)}, s32[1,16,8]{1,2,0:T(8,128)}, u32[]{:S(2)}) copy-start(s32[1,16,8]{1,2,0:T(8,128)} %param.14) | copy-start | bytes 1540
  439.9 14.7 %all-to-all-start.3 = ((bf16[128,16,128]{2,0,1:T(8,128)(2,1)}), bf16[128,16,128]{2,0,1:T(8,128)(2,1)}, u32[]{:S(2)}, u32[]{:S(2)}) async-start(bf16[128,16,128]{2,0,1:T(8,128)(2,1)} %bitcast.121), calls=%async_computation.3 | async-start | bytes 1048576 | tf_op jit(solution)/shard_map/all_to_all | solution.py:103
  458.2 3.7 copy-start.1
  471.7 3.0 copy-start.5
  488.6 3.7 copy-start.1
  502.0 3.0 copy-start.5
  518.9 3.7 copy-start.1
  532.4 3.0 copy-start.2
  532.4 3.0 copy-start.5
  549.3 3.7 copy-start.1
  562.7 3.0 copy-start.5
  577.3 6.2 copy-start.3
  579.9 13.7 %all-to-all-start.6 = ((bf16[16,2,8192]{2,1,0:T(2,128)(2,1)}), bf16[16,2,8192]{2,1,0:T(2,128)(2,1)S(1)}, u32[]{:S(2)}, u32[]{:S(2)}) async-start(bf16[16,2,8192]{2,1,0:T(2,128)(2,1)} %reshape.260), calls=%async_computation.6 | async-start | bytes 1048576 | tf_op jit(solution)/shard_map/all_to_all | solution.py:112
  593.6 13.7 %all-to-all-start.7 = ((bf16[16,2,8192]{2,1,0:T(2,128)(2,1)}), bf16[16,2,8192]{2,1,0:T(2,128)(2,1)S(1)}, u32[]{:S(2)}, u32[]{:S(2)}) async-start(bf16[16,2,8192]{2,1,0:T(2,128)(2,1)} %reshape.262), calls=%async_computation.7 | async-start | bytes 1048576 | tf_op jit(solution)/shard_map/all_to_all | solution.py:113
  607.3 13.7 %all-to-all-start.5 = ((bf16[16,2,8192]{2,1,0:T(2,128)(2,1)}), bf16[16,2,8192]{2,1,0:T(2,128)(2,1)S(1)}, u32[]{:S(2)}, u32[]{:S(2)}) async-start(bf16[16,2,8192]{2,1,0:T(2,128)(2,1)} %reshape.258), calls=%async_computation.5 | async-start | bytes 1048576 | tf_op jit(solution)/shard_map/all_to_all | solution.py:111
  (7 other events, 20.3 us)
